TPU v7x, 512 devices: a whole 4x8x8 slice. The times are simulated.
512 devices in a mesh: row: 16 (over y, core), col: 32 (over z, x).
Axes of the slice: x: 4, y: 8, z: 8, core: 2. Of those that a mesh axis runs over, the one named last changes fastest.
Arguments:
- matrix: float32 [4, 16, 256, 2, 32, 256], P(None, 'row', None, None, 'col'), as said below
- vectors: float32 [4, 16, 256, 256], P(None, 'row'), may hold values from -0.046875 to 0.046875
- t_factor: float32 [256, 256], replicated, as said below
Outputs:
- updated: float32 [4, 16, 256, 2, 32, 256], P(None, 'row', None, None, 'col')
Inputs may be any that keep to these rules, and one draw needn't show every extreme that they name: matrix is exactly symmetric as an 16384 x 16384 matrix: entry (i, j) equals entry (j, i). t_factor is upper triangular with its diagonal between 0.5 and 1.5.
All inputs are finite; a program needn't handle non-finite values.
Results may differ from a plain program's by a relative error of at most 0.000068.
Values sent between devices are 32-bit elements; how exact they have to be, the bound alone decides.
A program may use at most 64 MiB of HBM per device.

v0:
```python
import jax
import jax.numpy as jnp
from jax import lax
from jax.sharding import PartitionSpec as P


def spread(value, axis, root):
    mine = lax.axis_index(axis) == root
    return lax.psum(jnp.where(mine, value, jnp.zeros_like(value)), axis)


def product(left, right):
    return jnp.dot(left, right, precision=lax.Precision.HIGHEST, preferred_element_type=jnp.float32)


def per_device(matrix, vectors, t_factor):
    block_rows = vectors.shape[0]
    block_size = vectors.shape[2]
    block_cols = matrix.shape[3]
    row_devs = lax.axis_size("row")
    col_devs = lax.axis_size("col")
    col_ratio = col_devs // row_devs
    row_pos = lax.axis_index("row")
    col_pos = lax.axis_index("col")
    top_block = vectors[0, 0]
    unit_top = jnp.tril(top_block, -1) + jnp.eye(block_size, dtype=jnp.float32)
    first_block = jnp.where(row_pos == 0, unit_top, top_block)
    blocks = jnp.concatenate([first_block[None], vectors[1:, 0]], axis=0)
    chosen_ids = col_ratio * jnp.arange(block_cols, dtype=jnp.int32) + col_pos // row_devs
    source_row = col_pos % row_devs
    chosen = jnp.take(blocks, chosen_ids, axis=0)
    col_vecs = spread(chosen, "row", source_row).reshape(block_cols * block_size, block_size)
    row_vecs = blocks.reshape(block_rows * block_size, block_size)
    local_tile = matrix.reshape(block_rows * block_size, block_cols * block_size)
    summed = lax.psum(product(local_tile, col_vecs), "col")
    applied = product(summed, t_factor)
    inner = lax.psum(product(row_vecs.T, applied), "row")
    middle = product(t_factor.T, inner)
    coupled_rows = applied - 0.5 * product(row_vecs, middle)
    coupled_blocks = jnp.take(
        coupled_rows.reshape(block_rows, block_size, block_size), chosen_ids, axis=0
    )
    coupled_cols = spread(coupled_blocks, "row", source_row).reshape(
        block_cols * block_size, block_size
    )
    result = local_tile - product(row_vecs, coupled_cols.T) - product(coupled_rows, col_vecs.T)
    return result.reshape(matrix.shape)


def solution(mesh):
    in_specs = (P(None, "row", None, None, "col", None), P(None, "row", None, None), P())
    out_specs = P(None, "row", None, None, "col", None)
    return jax.shard_map(
        per_device, mesh=mesh, in_specs=in_specs, out_specs=out_specs, check_vma=False
    )
```

profile of v0, /device:TPU:1, one launch (start us, length us, event | category | flops | bytes accessed | tf_op | source)
XLA Modules:
  0.0 565.3 jit_solution(9547505962765150211)
XLA Ops:
  6.5 0.0 copy-start
  6.5 0.0 all-reduce.5.cloned.1.call-start
  6.6 1.2 slice_bitcast_fusion
  7.8 1.1 bitcast_select_fusion
  8.9 0.0 copy-start.3
  8.9 0.1 pad_maximum_fusion
  9.0 1.4 gather_fusion
  10.4 1.9 select_select_fusion.1
  12.3 0.0 all-reduce.5.cloned.1.call-update
  12.3 0.0 all-reduce.7.cloned.1.call-start
  12.4 0.0 copy-done.3
  12.4 8.1 %reduce = f32[4,256,2,256]{3,2,1,0:T(2,128)} reduce(f32[4,1,256,2,1,256]{5,4,3,2,1,0:T(1,128)S(1)} %copy-done.3, f32[]{:T(128)} %constant.58), dimensions={1,4}, to_apply=%param.5.reduce_sub_computation | reduce | bytes 4194308 | tf_op args[0]
  20.5 1.8 copy.5
  22.2 111.7 %all-reduce.5.cloned.1.call-done = f32[512,256]{1,0:T(8,128)} async-done(((f32[512,256]{1,0:T(8,128)}), f32[512,256]{1,0:T(8,128)}) %all-reduce.5.cloned.1.call-update) | async-done | bytes 524304 | tf_op jit(solution)/shard_map/psum | solution.py:9
  133.9 5.5 convolution_bitcast_fusion
  139.4 0.0 all-reduce.7.cloned.1.call-update
  139.4 0.2 all-reduce.9.cloned.1.call-start
  139.7 158.1 %all-reduce.7.cloned.1.call-done = f32[1024,256]{0,1:T(8,128)} async-done(((f32[1024,256]{0,1:T(8,128)}), f32[1024,256]{0,1:T(8,128)}) %all-reduce.7.cloned.1.call-update) | async-done | bytes 1048592 | tf_op jit(solution)/shard_map/psum | solution.py:35
  297.7 0.0 copy-done
  297.7 3.0 fusion.2
  300.8 0.0 copy-start.1
  300.8 1.0 copy-done.1
  301.7 2.5 fusion.3
  304.3 0.0 all-reduce.9.cloned.1.call-update
  304.3 0.0 all-reduce.11.cloned.1.call-start
  304.3 116.9 %all-reduce.9.cloned.1.call-done = f32[256,256]{1,0:T(8,128)} async-done(((f32[256,256]{1,0:T(8,128)}), f32[256,256]{1,0:T(8,128)}) %all-reduce.9.cloned.1.call-update) | async-done | bytes 262160 | tf_op jit(solution)/shard_map/psum | solution.py:37
  421.3 1.5 fusion.4
  422.8 3.2 fusion
  426.0 2.6 gather_fusion.1
  428.6 1.9 select_select_fusion
  430.6 0.0 all-reduce.11.cloned.1.call-update
  430.6 117.0 %all-reduce.11.cloned.1.call-done = f32[512,256]{1,0:T(8,128)} async-done(((f32[512,256]{1,0:T(8,128)}), f32[512,256]{1,0:T(8,128)}) %all-reduce.11.cloned.1.call-update) | async-done | bytes 524304 | tf_op jit(solution)/shard_map/psum | solution.py:9
  547.6 0.0 copy-start.2
  547.6 0.0 copy-start.4
  547.6 3.0 fusion.5
  550.6 0.0 copy-done.2
  550.7 0.0 copy-done.4
  550.7 3.4 subtract_subtract_fusion
  554.1 4.7 reshape.111
  (4 shorter events, 0.0 us)
Async XLA Ops:
  6.5 291.2 %copy-start = (f32[256,256]{1,0:T(8,128)S(1)}, f32[256,256]{1,0:T(8,128)}, u32[]{:S(2)}) copy-start(f32[256,256]{1,0:T(8,128)} %param.7) | copy-start | bytes 786436
  6.5 127.4 %all-reduce.5.cloned.1.call-start = ((), (), s32[]{:S(2)}) async-start(), calls=%async_computation | async-start | bytes 1048576 | tf_op jit(solution)/shard_map/psum | solution.py:9
  8.9 3.5 copy-start.3
  12.3 285.4 %all-reduce.7.cloned.1.call-start = ((), (), s32[]{:S(2)}) async-start(), calls=%async_computation.1 | async-start | bytes 2097152 | tf_op jit(solution)/shard_map/psum | solution.py:35
  139.4 281.8 %all-reduce.9.cloned.1.call-start = ((), (), s32[]{:S(2)}) async-start(), calls=%async_computation.2 | async-start | bytes 524288 | tf_op jit(solution)/shard_map/psum | solution.py:37
  300.8 1.0 copy-start.1
  304.3 243.3 %all-reduce.11.cloned.1.call-start = ((), (), s32[]{:S(2)}) async-start(), calls=%async_computation.3 | async-start | bytes 1048576 | tf_op jit(solution)/shard_map/psum | solution.py:9
  547.6 3.0 copy-start.2
  547.6 3.0 copy-start.4
Sparse Core Ops, SparseCore 0:
  12.5 121.3 all-reduce.4
  139.6 158.1 all-reduce.6
  304.4 116.7 all-reduce.8
  430.7 116.8 all-reduce.10
where the time goes:
time: 566 us; the launch traced here: 565 us
  waiting for transfers between devices  504 us (89%)
  matrix products  22.3 us (4%)
  between operations  13.3 us (2%)
  other arithmetic  13.1 us (2%)
  local copies, waits for them, and re-layouts  12.6 us (2%)
    psum x2, waiting for transfers between devices, spread(): return lax.psum(jnp.where(mine, value, jnp.zeros_like(value)), axis)  229 us
    psum x1, waiting for transfers between devices, per_device(): summed = lax.psum(product(local_tile, col_vecs), 'col')  158 us
    psum x1, waiting for transfers between devices, per_device(): inner = lax.psum(product(row_vecs.T, applied), 'row')  117 us
    dot_general x7, matrix products, product(): jnp.dot(left, right, precision=lax.Precision.HIGHEST, preferred_element_t...  22.3 us
  transfers between devices with their start and end apart: 4, of which 4 were waited for; matrix products, arithmetic and copies ran while one was open for 2% of the time, Pallas kernels for 0%

commit v1 on v0

--- a/solution.py
+++ b/solution.py
@@ -34,7 +34,7 @@
     local_tile = matrix.reshape(block_rows * block_size, block_cols * block_size)
     summed = lax.psum(product(local_tile, col_vecs), "col")
     applied = product(summed, t_factor)
-    inner = lax.psum(product(row_vecs.T, applied), "row")
+    inner = jnp.sum(lax.all_gather(product(row_vecs.T, applied), "row"), axis=0)
     middle = product(t_factor.T, inner)
     coupled_rows = applied - 0.5 * product(row_vecs, middle)
     coupled_blocks = jnp.take(

time: 566 us -> 496 us (0.88)
  waiting for transfers between devices: 504 us -> 430 us
    psum x1 -> x0, waiting for transfers between devices: 117 us -> none  [per_device(): inner = lax.psum(product(row_vecs.T, applied), 'row')]
    all_gather x0 -> x1, waiting for transfers between devices: none -> 46.5 us  [per_device(): inner = jnp.sum(lax.all_gather(product(row_vecs.T, applied), 'row'), axis=0)]
where the time goes in v1:
time: 496 us; the launch traced here: 495 us
  waiting for transfers between devices  430 us (87%)
  matrix products  22.2 us (4%)
  other arithmetic  16.3 us (3%)
  between operations  13.3 us (3%)
  local copies, waits for them, and re-layouts  12.6 us (3%)
    psum x2, waiting for transfers between devices, spread(): return lax.psum(jnp.where(mine, value, jnp.zeros_like(value)), axis)  226 us
    psum x1, waiting for transfers between devices, per_device(): summed = lax.psum(product(local_tile, col_vecs), 'col')  158 us
    all_gather x1, waiting for transfers between devices, per_device(): inner = jnp.sum(lax.all_gather(product(row_vecs.T, applied), 'row'), axis=0)  46.5 us
    dot_general x7, matrix products, product(): jnp.dot(left, right, precision=lax.Precision.HIGHEST, preferred_element_t...  22.2 us
  transfers between devices with their start and end apart: 4, of which 4 were waited for; matrix products, arithmetic and copies ran while one was open for 2% of the time, Pallas kernels for 0%

profile of v1, /device:TPU:1, one launch (start us, length us, event | category | flops | bytes accessed | tf_op | source)
XLA Modules:
  0.0 495.2 jit_solution(4810285379709199058)
XLA Ops:
  6.5 0.0 copy-start
  6.5 0.0 all-reduce.4.cloned.1.call-start
  6.6 1.2 slice_bitcast_fusion
  7.8 1.1 bitcast_select_fusion
  8.9 0.0 copy-start.3
  8.9 0.1 pad_maximum_fusion
  9.0 1.4 gather_fusion
  10.4 1.9 select_select_fusion.1
  12.3 0.0 all-reduce.4.cloned.1.call-update
  12.3 0.0 all-reduce.6.cloned.1.call-start
  12.4 0.0 copy-done.3
  12.4 8.1 %reduce = f32[4,256,2,256]{3,2,1,0:T(2,128)} reduce(f32[4,1,256,2,1,256]{5,4,3,2,1,0:T(1,128)S(1)} %copy-done.3, f32[]{:T(128)} %constant.59), dimensions={1,4}, to_apply=%param.5.reduce_sub_computation | reduce | bytes 4194308 | tf_op args[0]
  20.5 1.8 copy.5
  22.2 111.7 %all-reduce.4.cloned.1.call-done = f32[512,256]{1,0:T(8,128)} async-done(((f32[512,256]{1,0:T(8,128)}), f32[512,256]{1,0:T(8,128)}) %all-reduce.4.cloned.1.call-update) | async-done | bytes 524304 | tf_op jit(solution)/shard_map/psum | solution.py:9
  133.9 5.5 %convolution_bitcast_fusion = f32[1024,256]{0,1:T(8,128)} fusion(f32[512,256]{1,0:T(8,128)} %all-reduce.4.cloned.1.call-done, f32[1024,512]{1,0:T(8,128)S(1)} %bitcast.36), kind=kOutput, calls=%fused_computation.3 | convolution fusion | flops 1610612736 | bytes 3670016 | tf_op jit(solution)/shard_map/dot_general | solution.py:13
  139.4 0.0 all-reduce.6.cloned.1.call-update
  139.4 0.2 all-gather.3.cloned.1.call-start
  139.7 158.1 %all-reduce.6.cloned.1.call-done = f32[1024,256]{0,1:T(8,128)} async-done(((f32[1024,256]{0,1:T(8,128)}), f32[1024,256]{0,1:T(8,128)}) %all-reduce.6.cloned.1.call-update) | async-done | bytes 1048592 | tf_op jit(solution)/shard_map/psum | solution.py:35
  297.7 0.0 copy-done
  297.7 3.0 fusion.2
  300.8 0.0 copy-start.1
  300.8 1.0 copy-done.1
  301.7 2.5 fusion.3
  304.2 0.0 all-gather.3.cloned.1.call-update
  304.3 0.0 all-reduce.8.cloned.1.call-start
  304.3 46.5 %all-gather.3.cloned.1.call-done = f32[4096,256]{1,0:T(8,128)} async-done(((f32[256,256]{1,0:T(8,128)}), f32[4096,256]{1,0:T(8,128)}) %all-gather.3.cloned.1.call-update) | async-done | bytes 4194320 | tf_op jit(solution)/shard_map/all_gather | solution.py:37
  350.8 3.2 reduce_sum.9
  354.0 1.5 fusion.4
  355.5 3.2 fusion
  358.8 2.6 gather_fusion.1
  361.4 1.9 select_select_fusion
  363.3 0.0 all-reduce.8.cloned.1.call-update
  363.3 114.2 %all-reduce.8.cloned.1.call-done = f32[512,256]{1,0:T(8,128)} async-done(((f32[512,256]{1,0:T(8,128)}), f32[512,256]{1,0:T(8,128)}) %all-reduce.8.cloned.1.call-update) | async-done | bytes 524304 | tf_op jit(solution)/shard_map/psum | solution.py:9
  477.5 0.0 copy-start.2
  477.5 0.0 copy-start.4
  477.5 3.0 fusion.5
  480.6 0.0 copy-done.2
  480.6 0.0 copy-done.4
  480.6 3.4 subtract_subtract_fusion
  484.0 4.7 reshape.112
  (4 shorter events, 0.0 us)
Async XLA Ops:
  6.5 291.2 %copy-start = (f32[256,256]{1,0:T(8,128)S(1)}, f32[256,256]{1,0:T(8,128)}, u32[]{:S(2)}) copy-start(f32[256,256]{1,0:T(8,128)} %param.7) | copy-start | bytes 786436
  6.5 127.4 %all-reduce.4.cloned.1.call-start = ((), (), s32[]{:S(2)}) async-start(), calls=%async_computation | async-start | bytes 1048576 | tf_op jit(solution)/shard_map/psum | solution.py:9
  8.9 3.5 copy-start.3
  12.3 285.4 %all-reduce.6.cloned.1.call-start = ((), (), s32[]{:S(2)}) async-start(), calls=%async_computation.1 | async-start | bytes 2097152 | tf_op jit(solution)/shard_map/psum | solution.py:35
  139.4 211.4 %all-gather.3.cloned.1.call-start = ((), (), s32[]{:S(2)}) async-start(), calls=%async_computation.3 | async-start | bytes 4456448 | tf_op jit(solution)/shard_map/all_gather | solution.py:37
  300.8 1.0 copy-start.1
  304.3 173.3 %all-reduce.8.cloned.1.call-start = ((), (), s32[]{:S(2)}) async-start(), calls=%async_computation.2 | async-start | bytes 1048576 | tf_op jit(solution)/shard_map/psum | solution.py:9
  477.5 3.0 copy-start.2
  477.5 3.0 copy-start.4
Sparse Core Ops, SparseCore 0:
  12.5 121.3 all-reduce.3
  139.6 158.1 all-reduce.5
  304.4 46.3 all-gather.2
  363.4 114.0 all-reduce.7
